TPU v7x, 256 devices: a whole 4x4x8 slice. The times are simulated.
256 devices in a mesh: seq: 64 (over x, z, core), tp: 4 (over y).
Axes of the slice: x: 4, y: 4, z: 8, core: 2. Of those that a mesh axis runs over, the one named last changes fastest.
Arguments:
- token_ids: int32 [65536], P('seq'), may hold values from 0 to 511
- embed_table: bfloat16 [512, 2048], P(None, 'tp'), may hold values from -6 to 6
- norm_gain: float32 [2048], replicated, may hold values from 0.1 to 1.9
- in_weight: bfloat16 [2048, 3, 2048], P('seq', None, 'tp'), may hold values from -0.125 to 0.125
- short_filter: float32 [7, 3, 2048], P(None, None, 'tp'), may hold values from -2.4 to 2.4
- long_filter: bfloat16 [128, 128], P('tp'), may hold values from -0.5390625 to 0.5390625
- long_skip: float32 [2048], P('tp'), may hold values from -3 to 3
- out_weight: bfloat16 [2048, 2048], P('tp', 'seq'), may hold values from -0.125 to 0.125
Outputs:
- mixed: bfloat16 [65536, 2048], P('seq', 'tp')
All inputs are finite; a program needn't handle non-finite values.
Results may differ from a plain program's by a relative error of at most 0.012.
Values may be sent and summed in bfloat16 or wider, within the bound.
A program may use at most 64 MiB of HBM per device.

v0:
```python
import jax
import jax.numpy as jnp
from jax import lax
from jax.sharding import PartitionSpec as P


def from_behind(block, axis, distance):
    devices = range(lax.axis_size(axis))
    route = [(i - distance, i) for i in devices if i - distance in devices]
    return lax.ppermute(block, axis, route)


def short_conv(extended, short_filter, out_length):
    short_taps = short_filter.shape[0]
    running = jnp.zeros((out_length,) + extended.shape[1:], jnp.float32)
    for tap_index in range(short_taps):
        begin = short_taps - 1 - tap_index
        running = running + short_filter[tap_index][None] * extended[
            begin : begin + out_length
        ].astype(jnp.float32)
    return running


def body(
    token_ids, embed_table, norm_gain, in_weight, short_filter, long_filter, long_skip, out_weight
):
    tok_count = token_ids.shape[0]
    vocab_size = embed_table.shape[0]
    local_width = embed_table.shape[1]
    onehot = (token_ids[:, None] == jnp.arange(vocab_size, dtype=jnp.int32)[None, :]).astype(
        jnp.bfloat16
    )
    own_feats = jnp.dot(onehot, embed_table, preferred_element_type=jnp.float32).astype(
        jnp.bfloat16
    )
    features = lax.all_gather(own_feats, "tp", axis=1, tiled=True)
    widened = features.astype(jnp.float32)
    scaled = (
        widened
        * lax.rsqrt(jnp.mean(widened * widened, axis=1, keepdims=True) + 1e-06)
        * norm_gain[None, :]
    )
    normed = scaled.astype(jnp.bfloat16)
    projected = jnp.einsum(
        "td,dsc->tsc",
        normed,
        lax.all_gather(in_weight, "seq", axis=0, tiled=True),
        preferred_element_type=jnp.float32,
    ).astype(jnp.bfloat16)
    tap_count = long_filter.shape[1]
    short_taps = short_filter.shape[0]
    rim_rows = from_behind(projected[tok_count - short_taps + 1 :], "seq", 1)
    extended = jnp.concatenate([rim_rows, projected], axis=0)
    featured = short_conv(extended, short_filter, tok_count)
    queries = featured[:, 0]
    gated_kv = (featured[:, 1] * featured[:, 2]).astype(jnp.bfloat16)
    earlier = from_behind(gated_kv[tok_count - tap_count :], "seq", 1)
    product = jnp.concatenate([earlier, gated_kv], axis=0)
    groups_here = long_filter.shape[0]
    group_size = local_width // groups_here
    positions = jnp.arange(tap_count, dtype=jnp.int32)
    differ = positions[:, None, None] - positions[None, :, None]
    target = positions[None, None, :]
    near_pick = (differ == target).astype(jnp.float32)
    far_pick = (differ + tap_count == target).astype(jnp.float32)
    filter_f32 = long_filter.astype(jnp.float32)
    near_band = jnp.einsum("isj,gj->gis", near_pick, filter_f32).astype(jnp.bfloat16)
    far_band = jnp.einsum("isj,gj->gis", far_pick, filter_f32).astype(jnp.bfloat16)
    blocks = product.reshape(tok_count // tap_count + 1, tap_count, groups_here, group_size)
    convolved = jnp.einsum(
        "gis,bsgc->bigc", near_band, blocks[1:], preferred_element_type=jnp.float32
    )
    convolved = convolved + jnp.einsum(
        "gis,bsgc->bigc", far_band, blocks[:-1], preferred_element_type=jnp.float32
    )
    convolved = convolved.reshape(tok_count, local_width) + long_skip[None, :] * product[
        tap_count:
    ].astype(jnp.float32)
    gated = (queries * convolved).astype(jnp.bfloat16)
    partials = jnp.dot(
        gated,
        lax.all_gather(out_weight, "seq", axis=1, tiled=True),
        preferred_element_type=jnp.float32,
    )
    summed = lax.psum(partials.astype(jnp.bfloat16), "tp").astype(jnp.float32)
    own_share = lax.dynamic_slice_in_dim(summed, lax.axis_index("tp") * local_width, local_width, 1)
    return (own_feats.astype(jnp.float32) + own_share).astype(jnp.bfloat16)


def solution(mesh):
    placed = (
        P("seq"),
        P(None, "tp"),
        P(),
        P("seq", None, "tp"),
        P(None, None, "tp"),
        P("tp", None),
        P("tp"),
        P("tp", "seq"),
    )
    return jax.shard_map(
        body, mesh=mesh, in_specs=placed, out_specs=P("seq", "tp"), check_vma=False
    )
```

profile of v0, /device:TPU:1, one launch (start us, length us, event | category | flops | bytes accessed | tf_op | source)
XLA Modules:
  0.0 337.5 jit_solution(16231888260444834584)
XLA Ops:
  6.5 1.0 copy-done
  7.6 2.4 fusion.24
  10.1 0.7 all-gather.6.cloned.1.call-update
  10.8 0.7 all-gather.8.cloned.1.call-update
  11.6 1.2 fusion.38
  12.8 5.8 %fusion.3 = bf16[128,128,32]{1,2,0:T(8,128)(2,1)} fusion(s32[128,128]{1,0:T(8,128)S(1)} %iota_subtract_fusion, bf16[32,128]{1,0:T(8,128)(2,1)} %param.13), kind=kOutput, calls=%fused_computation.7 | convolution fusion | flops 136314880 | bytes 1122304 | tf_op jit(solution)/shard_map/isj,gj->gis/dot_general | solution.py:67
  18.6 5.1 %fusion.4 = bf16[128,128,32]{1,2,0:T(8,128)(2,1)} fusion(s32[128,128]{1,0:T(8,128)S(1)} %broadcast_add_fusion, bf16[32,128]{1,0:T(8,128)(2,1)S(1)} %copy-done.5), kind=kOutput, calls=%fused_computation.8 | convolution fusion | flops 136314880 | bytes 1122304 | tf_op jit(solution)/shard_map/isj,gj->gis/dot_general | solution.py:68
  23.7 40.8 %all-gather.4.cloned.1.call-done = bf16[1024,2048]{1,0:T(8,128)(2,1)} async-done(((bf16[1024,512]{1,0:T(8,128)(2,1)}), bf16[1024,2048]{1,0:T(8,128)(2,1)}) %all-gather.4.cloned.1.call-update) | async-done | bytes 4194320 | tf_op jit(solution)/shard_map/all_gather | solution.py:36
  64.6 3.1 fusion
  67.7 81.2 %all-gather.6.cloned.1.call-done = bf16[2048,3,512]{2,0,1:T(8,128)(2,1)} async-done(((bf16[32,3,512]{2,0,1:T(8,128)(2,1)}), bf16[2048,3,512]{2,0,1:T(8,128)(2,1)}) %all-gather.6.cloned.1.call-update) | async-done | bytes 6291472 | tf_op jit(solution)/shard_map/all_gather | solution.py:47
  148.8 10.5 %fusion.17 = bf16[1024,3,512]{2,0,1:T(8,128)(2,1)S(1)} fusion(bf16[2048,3,512]{2,0,1:T(8,128)(2,1)} %all-gather.6.cloned.1.call-done, bf16[1024,2048]{1,0:T(8,128)(2,1)} %all-gather.4.cloned.1.call-done, f32[2048]{0:T(1024)S(1)} %copy-done.6, f32[1024]{0:T(1024)S(1)} %add_rsqrt_fusion), kind=kOutput, calls=%fused_computation.31 | convolution fusion | flops 6452412416 | bytes 13643776 | tf_op jit(solution)/shard_map/td,dsc->tsc/dot_general | solution.py:44
  159.4 2.8 collective-permute-start
  162.2 0.9 collective-permute-done
  163.1 5.6 %multiply_add_fusion = f32[1024,3,512]{2,0,1:T(8,128)S(1)} fusion(bf16[1024,3,512]{2,0,1:T(8,128)(2,1)S(1)} %fusion.17, bf16[6,3,512]{2,0,1:T(8,128)(2,1)S(1)} %collective-permute-done, f32[3,512]{1,0:T(4,128)S(1)} %get-tuple-element.12, f32[3,512]{1,0:T(4,128)S(1)} %get-tuple-element.13, f32[3,512]{1,0:T(4,128)S(1)} %get-tuple-element.14, ...), kind=kLoop, calls=%fused_computation.14 | loop fusion | flops 59768832 | bytes 9498624 | tf_op jit(solution)/shard_map/add | solution.py:18
  168.7 2.7 copy-done.1
  171.3 0.4 fusion.20
  171.7 0.5 copy.12
  172.3 4.7 %collective-permute-start.1 = (bf16[128,512]{1,0:T(8,128)(2,1)S(1)}, bf16[128,512]{1,0:T(8,128)(2,1)S(1)}, u32[]{:S(2)}, u32[]{:S(2)}) collective-permute-start(bf16[128,512]{1,0:T(8,128)(2,1)S(1)} %slice_bitcast_fusion.1), channel_id=1, source_target_pairs={{0,4},{4,8},{8,12},{12,16},{16,20},{20,24},{24,28},{28,32},{32,36}... | collective-permute-start | bytes 393224 | tf_op jit(solution)/shard_map/ppermute | solution.py:10
  176.9 0.3 copy.29
  177.2 2.1 fusion.26
  179.3 0.4 fusion.42
  179.7 1.1 pad_maximum_fusion.1
  180.7 2.3 copy.14
  183.0 1.5 copy.30
  184.5 2.1 add_bitcast_fusion
  186.6 0.9 copy.16
  187.5 0.5 copy.52
  188.0 1.8 copy.17
  189.8 35.9 %all-gather.8.cloned.1.call-done = bf16[512,2048]{0,1:T(8,128)(2,1)} async-done(((bf16[512,32]{0,1:T(8,128)(2,1)}), bf16[512,2048]{0,1:T(8,128)(2,1)}) %all-gather.8.cloned.1.call-update) | async-done | bytes 2097168 | tf_op jit(solution)/shard_map/all_gather | solution.py:82
  225.7 7.6 %convolution_convert_fusion = bf16[1024,2048]{1,0:T(8,128)(2,1)} fusion(bf16[512,2048]{0,1:T(8,128)(2,1)} %all-gather.8.cloned.1.call-done, f32[1024,3,512]{2,0,1:T(8,128)} %copy-done.1, f32[1024,512]{1,0:T(8,128)} %copy.17, f32[512]{0:T(512)S(1)} %copy-done.7, bf16[1024,1,512]{2,0,1:T(8,128)(2,1)} %copy-done.3), kind=kOutput, calls=%fused_computation.21 | convolution fusion | flops 2152202240 | bytes 11536384 | tf_op jit(solution)/shard_map/dot_general | solution.py:80
  233.3 95.2 %all-reduce.2.cloned.1.call-done = bf16[1024,2048]{1,0:T(8,128)(2,1)} async-done(((bf16[1024,2048]{1,0:T(8,128)(2,1)}), bf16[1024,2048]{1,0:T(8,128)(2,1)}) %all-reduce.2.cloned.1.call-update) | async-done | bytes 4194320 | tf_op jit(solution)/shard_map/psum | solution.py:85
  328.5 2.5 add_convert_fusion
  (30 shorter events, 0.3 us)
Async XLA Ops:
  6.5 1.0 copy-start
  6.5 12.1 %copy-start.5 = (bf16[32,128]{1,0:T(8,128)(2,1)S(1)}, bf16[32,128]{1,0:T(8,128)(2,1)}, u32[]{:S(2)}) copy-start(bf16[32,128]{1,0:T(8,128)(2,1)} %param.13) | copy-start | bytes 24580
  6.5 58.0 %all-gather.4.cloned.1.call-start = ((), (), s32[]{:S(2)}) async-start(), calls=%async_computation | async-start | bytes 5242880 | tf_op jit(solution)/shard_map/all_gather | solution.py:36
  10.0 138.8 %all-gather.6.cloned.1.call-start = ((), (), s32[]{:S(2)}) async-start(), calls=%async_computation.1 | async-start | bytes 6389760 | tf_op jit(solution)/shard_map/all_gather | solution.py:47
  10.8 214.9 %all-gather.8.cloned.1.call-start = ((), (), s32[]{:S(2)}) async-start(), calls=%async_computation.2 | async-start | bytes 2129920 | tf_op jit(solution)/shard_map/all_gather | solution.py:82
  11.5 317.0 %all-reduce.2.cloned.1.call-start = ((), (), s32[]{:S(2)}) async-start(), calls=%async_computation.3 | async-start | bytes 8388608 | tf_op jit(solution)/shard_map/psum | solution.py:85
  12.8 136.0 %copy-start.6 = (f32[2048]{0:T(1024)S(1)}, f32[2048]{0:T(1024)}, u32[]{:S(2)}) copy-start(f32[2048]{0:T(1024)} %param.10) | copy-start | bytes 24580
  159.4 3.7 %collective-permute-start = (bf16[6,3,512]{2,0,1:T(8,128)(2,1)S(1)}, bf16[6,3,512]{2,0,1:T(8,128)(2,1)S(1)}, u32[]{:S(2)}, u32[]{:S(2)}) collective-permute-start(bf16[6,3,512]{2,0,1:T(8,128)(2,1)S(1)} %slice.86), channel_id=1, source_target_pairs={{0,4},{4,8},{8,12},{12,16},{16,20},{20,24},{24,28},{28,32},{32,36}... | collective-permute-start | bytes 55304 | tf_op jit(solution)/shard_map/ppermute | solution.py:10
  168.7 2.7 copy-start.1
  171.7 5.5 %copy-start.3 = (bf16[1024,1,512]{2,0,1:T(8,128)(2,1)}, bf16[1024,1,512]{2,0,1:T(8,128)(2,1)S(1)}, u32[]{:S(2)}) copy-start(bf16[1024,1,512]{2,0,1:T(8,128)(2,1)S(1)} %fusion.20) | copy-start | bytes 3145732
  172.2 7.1 %copy-start.2 = (f32[1024,3,512]{2,0,1:T(8,128)S(1)}, f32[1024,3,512]{2,0,1:T(8,128)}, u32[]{:S(2)}) copy-start(f32[1024,3,512]{2,0,1:T(8,128)} %copy-done.1) | copy-start | bytes 18874372
  172.3 7.4 %collective-permute-start.1 = (bf16[128,512]{1,0:T(8,128)(2,1)S(1)}, bf16[128,512]{1,0:T(8,128)(2,1)S(1)}, u32[]{:S(2)}, u32[]{:S(2)}) collective-permute-start(bf16[128,512]{1,0:T(8,128)(2,1)S(1)} %slice_bitcast_fusion.1), channel_id=1, source_target_pairs={{0,4},{4,8},{8,12},{12,16},{16,20},{20,24},{24,28},{28,32},{32,36}... | collective-permute-start | bytes 393224 | tf_op jit(solution)/shard_map/ppermute | solution.py:10
  186.6 39.1 %copy-start.7 = (f32[512]{0:T(512)S(1)}, f32[512]{0:T(512)}, u32[]{:S(2)}) copy-start(f32[512]{0:T(512)} %param.14) | copy-start | bytes 6148
  189.8 138.7 %copy-start.4 = (bf16[1024,512]{1,0:T(8,128)(2,1)S(1)}, bf16[1024,512]{1,0:T(8,128)(2,1)}, u32[]{:S(2)}) copy-start(bf16[1024,512]{1,0:T(8,128)(2,1)} %fusion.24) | copy-start | bytes 3145732
Sparse Core Ops, SparseCore 0:
  10.1 54.3 all-gather.3
  67.4 81.3 all-gather.5
  151.6 74.0 all-gather.7
  233.4 94.9 all-reduce.1
where the time goes:
time: 338 us; the launch traced here: 337 us
  waiting for transfers between devices  255 us (75%)
  matrix products  35.6 us (11%)
  between operations  13.3 us (4%)
  other arithmetic  12.9 us (4%)
  local copies, waits for them, and re-layouts  12.7 us (4%)
  starting transfers between devices  7.53 us (2%)
    psum x1, waiting for transfers between devices, body(): summed = lax.psum(partials.astype(jnp.bfloat16), 'tp').astype(jnp.float32)  95.2 us
    all_gather x1, waiting for transfers between devices, body(): lax.all_gather(in_weight, 'seq', axis=0, tiled=True)  81.2 us
    all_gather x1, waiting for transfers between devices, body(): features = lax.all_gather(own_feats, 'tp', axis=1, tiled=True)  40.8 us
    all_gather x1, waiting for transfers between devices, body(): lax.all_gather(out_weight, 'seq', axis=1, tiled=True)  35.9 us
    dot_general x1, matrix products, body(): jnp.einsum('td,dsc->tsc', normed, lax.all_gather(in_weight, 'seq', axis=0...  10.5 us
    dot_general x1, matrix products, body(): jnp.dot(gated, lax.all_gather(out_weight, 'seq', axis=1, tiled=True), pre...  7.59 us
    ppermute x2, starting transfers between devices, from_behind(): return lax.ppermute(block, axis, route)  7.41 us
  transfers between devices with their start and end apart: 6, of which 5 were waited for; matrix products, arithmetic and copies ran while one was open for 13% of the time, Pallas kernels for 0%

commit v1 on v0

--- a/solution.py
+++ b/solution.py
@@ -2,6 +2,7 @@
 import jax.numpy as jnp
 from jax import lax
 from jax.sharding import PartitionSpec as P
+from jax.lax import all_to_all, axis_size
 
 
 def from_behind(block, axis, distance):
@@ -77,10 +78,11 @@
         tap_count:
     ].astype(jnp.float32)
     gated = (queries * convolved).astype(jnp.bfloat16)
+    supply_all_types = lambda dev_axis, block_in: jnp.concatenate(
+        all_to_all(jnp.stack([block_in] * axis_size(dev_axis)), dev_axis, 0, 0), axis=1
+    )
     partials = jnp.dot(
-        gated,
-        lax.all_gather(out_weight, "seq", axis=1, tiled=True),
-        preferred_element_type=jnp.float32,
+        gated, supply_all_types("seq", out_weight), preferred_element_type=jnp.float32
     )
     summed = lax.psum(partials.astype(jnp.bfloat16), "tp").astype(jnp.float32)
     own_share = lax.dynamic_slice_in_dim(summed, lax.axis_index("tp") * local_width, local_width, 1)

time: 338 us -> 306 us (0.905)
  waiting for transfers between devices: 255 us -> 208 us
  starting transfers between devices: 7.53 us -> 20.6 us
  local copies, waits for them, and re-layouts: 12.7 us -> 16.1 us
    all_gather x1 -> x0, waiting for transfers between devices: 35.9 us -> none  [body(): lax.all_gather(out_weight, 'seq', axis=1, tiled=True)]
    all_to_all x0 -> x1, starting transfers between devices: none -> 13.2 us  [body(): all_to_all(jnp.stack([block_in] * axis_size(dev_axis)), dev_axis, 0, 0)]
    all_gather x1, waiting for transfers between devices: 40.8 us -> 27.9 us  [body(): features = lax.all_gather(own_feats, 'tp', axis=1, tiled=True)]
  transfers between devices with their start and end apart: 6 -> 6, of which waited for: 5 -> 4; matrix products, arithmetic and copies ran while one was open for 13% -> 16% of each run, Pallas kernels for 0% -> 0%
where the time goes in v1:
time: 306 us
  waiting for transfers between devices  208 us (68%)
  matrix products  34.6 us (11%)
  starting transfers between devices  20.6 us (7%)
  local copies, waits for them, and re-layouts  16.1 us (5%)
  between operations  13.4 us (4%)
  other arithmetic  12.9 us (4%)
    psum x1, waiting for transfers between devices, body(): summed = lax.psum(partials.astype(jnp.bfloat16), 'tp').astype(jnp.float32)  97.2 us
    all_gather x1, waiting for transfers between devices, body(): lax.all_gather(in_weight, 'seq', axis=0, tiled=True)  81.2 us
    all_gather x1, waiting for transfers between devices, body(): features = lax.all_gather(own_feats, 'tp', axis=1, tiled=True)  27.9 us
    all_to_all x1, starting transfers between devices, body(): all_to_all(jnp.stack([block_in] * axis_size(dev_axis)), dev_axis, 0, 0)  13.2 us
    dot_general x1, matrix products, body(): jnp.einsum('td,dsc->tsc', normed, lax.all_gather(in_weight, 'seq', axis=0...  10.5 us
    ppermute x2, starting transfers between devices, from_behind(): return lax.ppermute(block, axis, route)  7.39 us
    dot_general x1, matrix products, body(): jnp.dot(gated, supply_all_types('seq', out_weight), preferred_element_typ...  7.3 us
  transfers between devices with their start and end apart: 6, of which 4 were waited for; matrix products, arithmetic and copies ran while one was open for 16% of the time, Pallas kernels for 0%

profile of v1, /device:TPU:1, one launch (start us, length us, event | category | flops | bytes accessed | tf_op | source)
XLA Modules:
  0.0 305.5 jit_solution(14422530721791581817)
XLA Ops:
  6.5 1.0 copy-done
  7.6 2.4 fusion.23
  10.1 0.7 all-gather.5.cloned.1.call-update
  10.8 2.4 stack.2
  13.1 13.2 %all-to-all-start = ((bf16[64,512,32]{1,2,0:T(8,128)(2,1)}), bf16[64,512,32]{1,2,0:T(8,128)(2,1)}, u32[]{:S(2)}, u32[]{:S(2)}) async-start(bf16[64,512,32]{1,2,0:T(8,128)(2,1)} %stack.2), calls=%async_computation | async-start | bytes 4194304 | tf_op jit(solution)/shard_map/all_to_all | solution.py:82
  26.3 0.0 all-reduce.2.cloned.1.call-start
  26.5 5.1 %fusion.3 = bf16[128,128,32]{1,2,0:T(8,128)(2,1)} fusion(s32[128,128]{1,0:T(8,128)S(1)} %iota_subtract_fusion, bf16[32,128]{1,0:T(8,128)(2,1)S(1)} %copy-done.7), kind=kOutput, calls=%fused_computation.7 | convolution fusion | flops 136314880 | bytes 1122304 | tf_op jit(solution)/shard_map/isj,gj->gis/dot_general | solution.py:68
  31.6 5.1 %fusion.4 = bf16[128,128,32]{1,2,0:T(8,128)(2,1)} fusion(s32[128,128]{1,0:T(8,128)S(1)} %broadcast_add_fusion, bf16[32,128]{1,0:T(8,128)(2,1)S(1)} %copy-done.7), kind=kOutput, calls=%fused_computation.8 | convolution fusion | flops 136314880 | bytes 1122304 | tf_op jit(solution)/shard_map/isj,gj->gis/dot_general | solution.py:69
  36.7 27.9 %all-gather.3.cloned.1.call-done = bf16[1024,2048]{1,0:T(8,128)(2,1)} async-done(((bf16[1024,512]{1,0:T(8,128)(2,1)}), bf16[1024,2048]{1,0:T(8,128)(2,1)}) %all-gather.3.cloned.1.call-update) | async-done | bytes 4194320 | tf_op jit(solution)/shard_map/all_gather | solution.py:37
  64.6 3.1 %fusion = f32[1024]{0:T(1024)S(1)} fusion(bf16[1024,2048]{1,0:T(8,128)(2,1)} %all-gather.3.cloned.1.call-done), kind=kLoop, calls=%fused_computation.2 | loop fusion | flops 6290432 | bytes 4198400 | tf_op jit(solution)/shard_map/reduce_sum | solution.py:41
  67.7 81.2 %all-gather.5.cloned.1.call-done = bf16[2048,3,512]{2,0,1:T(8,128)(2,1)} async-done(((bf16[32,3,512]{2,0,1:T(8,128)(2,1)}), bf16[2048,3,512]{2,0,1:T(8,128)(2,1)}) %all-gather.5.cloned.1.call-update) | async-done | bytes 6291472 | tf_op jit(solution)/shard_map/all_gather | solution.py:48
  148.8 10.5 %fusion.17 = bf16[1024,3,512]{2,0,1:T(8,128)(2,1)S(1)} fusion(bf16[2048,3,512]{2,0,1:T(8,128)(2,1)} %all-gather.5.cloned.1.call-done, bf16[1024,2048]{1,0:T(8,128)(2,1)} %all-gather.3.cloned.1.call-done, f32[2048]{0:T(1024)S(1)} %copy-done.8, f32[1024]{0:T(1024)S(1)} %add_rsqrt_fusion), kind=kOutput, calls=%fused_computation.31 | convolution fusion | flops 6452412416 | bytes 13643776 | tf_op jit(solution)/shard_map/td,dsc->tsc/dot_general | solution.py:45
  159.4 2.7 collective-permute-start
  162.2 0.9 collective-permute-done
  163.1 5.6 %multiply_add_fusion = f32[1024,3,512]{2,0,1:T(8,128)S(1)} fusion(bf16[1024,3,512]{2,0,1:T(8,128)(2,1)S(1)} %fusion.17, bf16[6,3,512]{2,0,1:T(8,128)(2,1)S(1)} %collective-permute-done, f32[3,512]{1,0:T(4,128)S(1)} %get-tuple-element.12, f32[3,512]{1,0:T(4,128)S(1)} %get-tuple-element.13, f32[3,512]{1,0:T(4,128)S(1)} %get-tuple-element.14, ...), kind=kLoop, calls=%fused_computation.14 | loop fusion | flops 59768832 | bytes 9498624 | tf_op jit(solution)/shard_map/add | solution.py:19
  168.7 2.7 copy-done.1
  171.3 0.4 fusion.20
  171.7 0.5 copy.13
  172.3 4.7 %collective-permute-start.1 = (bf16[128,512]{1,0:T(8,128)(2,1)S(1)}, bf16[128,512]{1,0:T(8,128)(2,1)S(1)}, u32[]{:S(2)}, u32[]{:S(2)}) collective-permute-start(bf16[128,512]{1,0:T(8,128)(2,1)S(1)} %slice_bitcast_fusion), channel_id=1, source_target_pairs={{0,4},{4,8},{8,12},{12,16},{16,20},{20,24},{24,28},{28,32},{32,36}... | collective-permute-start | bytes 393224 | tf_op jit(solution)/shard_map/ppermute | solution.py:11
  176.9 0.3 copy.30
  177.2 2.1 fusion.25
  179.3 0.4 fusion.41
  179.7 1.1 pad_maximum_fusion.1
  180.7 2.3 copy.15
  183.0 1.5 copy.31
  184.5 2.1 add_bitcast_fusion
  186.6 0.9 copy.17
  187.5 1.5 reshape.65
  189.0 3.0 copy.18
  192.0 7.3 %convolution_convert_fusion = bf16[1024,2048]{1,0:T(8,128)(2,1)} fusion(bf16[512,2048]{0,1:T(8,128)(2,1)} %bitcast.13, f32[1024,1,512]{2,0,1:T(8,128)} %copy.18, bf16[1024,1,512]{2,0,1:T(8,128)(2,1)S(1)} %copy-done.4, f32[1024,3,512]{2,0,1:T(8,128)} %copy-done.1, f32[512]{0:T(512)S(1)} %copy-done.9), kind=kOutput, calls=%fused_computation.21 | convolution fusion | flops 2152202240 | bytes 11536384 | tf_op jit(solution)/shard_map/dot_general | solution.py:84
  199.3 97.2 %all-reduce.2.cloned.1.call-done = bf16[1024,2048]{1,0:T(8,128)(2,1)} async-done(((bf16[1024,2048]{1,0:T(8,128)(2,1)}), bf16[1024,2048]{1,0:T(8,128)(2,1)}) %all-reduce.2.cloned.1.call-update) | async-done | bytes 4194320 | tf_op jit(solution)/shard_map/psum | solution.py:87
  296.5 2.5 add_convert_fusion
  (34 shorter events, 0.2 us)
Async XLA Ops:
  6.5 1.0 copy-start
  6.5 58.0 %all-gather.3.cloned.1.call-start = ((), (), s32[]{:S(2)}) async-start(), calls=%async_computation.1 | async-start | bytes 5242880 | tf_op jit(solution)/shard_map/all_gather | solution.py:37
  10.0 16.4 %copy-start.6 = (f32[7,3,512]{2,0,1:T(8,128)S(1)}, f32[7,3,512]{2,0,1:T(8,128)}, u32[]{:S(2)}) copy-start(f32[7,3,512]{2,0,1:T(8,128)} %param.12) | copy-start | bytes 129028
  10.0 16.5 %copy-start.7 = (bf16[32,128]{1,0:T(8,128)(2,1)S(1)}, bf16[32,128]{1,0:T(8,128)(2,1)}, u32[]{:S(2)}) copy-start(bf16[32,128]{1,0:T(8,128)(2,1)} %param.13) | copy-start | bytes 24580
  10.0 138.8 %all-gather.5.cloned.1.call-start = ((), (), s32[]{:S(2)}) async-start(), calls=%async_computation.2 | async-start | bytes 6389760 | tf_op jit(solution)/shard_map/all_gather | solution.py:48
  13.1 178.9 %all-to-all-start = ((bf16[64,512,32]{1,2,0:T(8,128)(2,1)}), bf16[64,512,32]{1,2,0:T(8,128)(2,1)}, u32[]{:S(2)}, u32[]{:S(2)}) async-start(bf16[64,512,32]{1,2,0:T(8,128)(2,1)} %stack.2), calls=%async_computation | async-start | bytes 4194304 | tf_op jit(solution)/shard_map/all_to_all | solution.py:82
  26.3 270.2 %all-reduce.2.cloned.1.call-start = ((), (), s32[]{:S(2)}) async-start(), calls=%async_computation.3 | async-start | bytes 8388608 | tf_op jit(solution)/shard_map/psum | solution.py:87
  31.6 117.2 %copy-start.8 = (f32[2048]{0:T(1024)S(1)}, f32[2048]{0:T(1024)}, u32[]{:S(2)}) copy-start(f32[2048]{0:T(1024)} %param.10) | copy-start | bytes 24580
  159.4 3.7 %collective-permute-start = (bf16[6,3,512]{2,0,1:T(8,128)(2,1)S(1)}, bf16[6,3,512]{2,0,1:T(8,128)(2,1)S(1)}, u32[]{:S(2)}, u32[]{:S(2)}) collective-permute-start(bf16[6,3,512]{2,0,1:T(8,128)(2,1)S(1)} %slice.86), channel_id=1, source_target_pairs={{0,4},{4,8},{8,12},{12,16},{16,20},{20,24},{24,28},{28,32},{32,36}... | collective-permute-start | bytes 55304 | tf_op jit(solution)/shard_map/ppermute | solution.py:11
  168.7 2.7 copy-start.1
  171.7 5.5 %copy-start.3 = (bf16[1024,1,512]{2,0,1:T(8,128)(2,1)}, bf16[1024,1,512]{2,0,1:T(8,128)(2,1)S(1)}, u32[]{:S(2)}) copy-start(bf16[1024,1,512]{2,0,1:T(8,128)(2,1)S(1)} %fusion.20) | copy-start | bytes 3145732
  172.2 7.1 %copy-start.2 = (f32[1024,3,512]{2,0,1:T(8,128)S(1)}, f32[1024,3,512]{2,0,1:T(8,128)}, u32[]{:S(2)}) copy-start(f32[1024,3,512]{2,0,1:T(8,128)} %copy-done.1) | copy-start | bytes 18874372
  172.3 7.4 %collective-permute-start.1 = (bf16[128,512]{1,0:T(8,128)(2,1)S(1)}, bf16[128,512]{1,0:T(8,128)(2,1)S(1)}, u32[]{:S(2)}, u32[]{:S(2)}) collective-permute-start(bf16[128,512]{1,0:T(8,128)(2,1)S(1)} %slice_bitcast_fusion), channel_id=1, source_target_pairs={{0,4},{4,8},{8,12},{12,16},{16,20},{20,24},{24,28},{28,32},{32,36}... | collective-permute-start | bytes 393224 | tf_op jit(solution)/shard_map/ppermute | solution.py:11
  187.5 4.5 %copy-start.9 = (f32[512]{0:T(512)S(1)}, f32[512]{0:T(512)}, u32[]{:S(2)}) copy-start(f32[512]{0:T(512)} %param.14) | copy-start | bytes 6148
  189.0 3.0 copy-start.4
  199.3 97.2 %copy-start.5 = (bf16[1024,512]{1,0:T(8,128)(2,1)S(1)}, bf16[1024,512]{1,0:T(8,128)(2,1)}, u32[]{:S(2)}) copy-start(bf16[1024,512]{1,0:T(8,128)(2,1)} %fusion.23) | copy-start | bytes 3145732
Sparse Core Ops, SparseCore 0:
  10.1 54.3 all-gather.2
  67.4 81.4 all-gather.4
  199.5 97.0 all-reduce.1
